TPU v7x, 256 devices: a whole 4x4x8 slice. The times are simulated.
256 devices in a mesh: grp: 16 (over z, core), head: 16 (over y, x).
Axes of the slice: x: 4, y: 4, z: 8, core: 2. Of those that a mesh axis runs over, the one named last changes fastest.
Arguments:
- query_rows: bfloat16 [256, 128, 2048], P(('grp', 'head')), may hold values from -6 to 6
- key_rows: bfloat16 [256, 128, 2048], P(('grp', 'head')), may hold values from -6 to 6
- value_rows: bfloat16 [256, 128, 2048], P(('grp', 'head')), may hold values from -6 to 6
- log_decay: bfloat16 [256, 128, 2048], P(('grp', 'head')), may hold values from -1.5 to 0, as said below
- beta_logit: bfloat16 [256, 128, 16], P(('grp', 'head')), may hold values from -6 to 6
- out_grad: bfloat16 [256, 128, 2048], P(('grp', 'head')), may hold values from -6 to 6
- fork_state: float32 [8, 16, 128, 128], P(None, 'head'), may hold values from -6 to 6
- branch_prompt: int32 [256], replicated, may hold values from 0 to 7, as said below
- valid_len: int32 [256], replicated, may hold values from 32 to 128, as said below
Outputs:
- grad_query: bfloat16 [256, 128, 2048], P(('grp', 'head'))
- grad_key: bfloat16 [256, 128, 2048], P(('grp', 'head'))
- grad_value: bfloat16 [256, 128, 2048], P(('grp', 'head'))
- grad_decay: bfloat16 [256, 128, 2048], P(('grp', 'head'))
- grad_beta: bfloat16 [256, 128, 16], P(('grp', 'head'))
- grad_fork: float32 [8, 16, 128, 128], P(None, 'head')
Inputs may be any that keep to these rules, and one draw needn't show every extreme that they name: `log_decay`: never positive; a few tokens of each branch lose a large share of every channel at once. `branch_prompt`: every prompt has at least one branch. A branch counts its first valid_len tokens; some branch uses all 128.
All inputs are finite; a program needn't handle non-finite values.
Results may differ from a plain program's by a relative error of at most 0.0015.
Values may be sent and summed in bfloat16 or wider, within the bound.
A program may use at most 64 MiB of HBM per device.

v0:
```python
from functools import partial

import jax
import jax.numpy as jnp
from jax import lax
from jax.sharding import PartitionSpec as P


def decay_forward(query_in, key_in, value_in, decay_in, beta_in, state_in, keep_mask, block_len):
    head_dim = query_in.shape[-1]
    upper_limit = lax.Precision.HIGHEST
    unit_query = (
        query_in
        * lax.rsqrt(jnp.sum(query_in * query_in, axis=-1, keepdims=True) + 1e-06)
        * head_dim ** (-0.5)
    )
    unit_key = key_in * lax.rsqrt(jnp.sum(key_in * key_in, axis=-1, keepdims=True) + 1e-06)
    beta_value = jax.nn.sigmoid(beta_in) * keep_mask[None, :]
    decay_value = decay_in * keep_mask[None, :, None]
    token_positions = jnp.arange(block_len, dtype=jnp.int32)
    lower_strict = (token_positions[:, None] > token_positions[None, :]).astype(jnp.float32)
    lower_closed = (token_positions[:, None] >= token_positions[None, :]).astype(jnp.float32)
    identity_block = jnp.eye(block_len, dtype=jnp.float32)
    cum_decay = jnp.cumsum(decay_value, axis=1)
    growth = jnp.exp(cum_decay)
    shrink = jnp.exp(-cum_decay)
    key_forward_rows = unit_key * growth
    key_earlier_rows = unit_key * shrink
    query_forward_rows = unit_query * growth
    coupling = (
        jnp.einsum("htk,hsk->hts", key_forward_rows, key_earlier_rows, precision=upper_limit)
        * beta_value[:, :, None]
        * lower_strict
    )
    attend_scores = (
        jnp.einsum("htk,hsk->hts", query_forward_rows, key_earlier_rows, precision=upper_limit)
        * lower_closed
    )
    target_output = beta_value[:, :, None] * (
        value_in - jnp.einsum("led,ldf->lef", key_forward_rows, state_in, precision=upper_limit)
    )
    state_update = jax.scipy.linalg.solve_triangular(
        identity_block + coupling, target_output, lower=True, unit_diagonal=True
    )
    output_block_rows = jnp.einsum(
        "led,ldf->lef", query_forward_rows, state_in, precision=upper_limit
    ) + jnp.einsum("ifj,ijo->ifo", attend_scores, state_update, precision=upper_limit)
    outputs = [output_block_rows]
    return jnp.concatenate(outputs, axis=1)


def branch_backward(
    query_rows, key_rows, value_rows, log_decay, out_grad, beta_logit, states, valid_rows, block_len
):
    count, window_len, row_width = query_rows.shape
    heads_here = states.shape[1]
    head_dim = states.shape[-1]

    def split_heads(array_in):
        return (
            array_in.astype(jnp.float32)
            .reshape(count, window_len, heads_here, head_dim)
            .transpose(0, 2, 1, 3)
        )

    def join_heads(array_in):
        return (
            array_in.transpose(0, 2, 1, 3)
            .reshape(count, window_len, row_width)
            .astype(jnp.bfloat16)
        )

    keep_mask = (jnp.arange(window_len, dtype=jnp.int32)[None, :] < valid_rows[:, None]).astype(
        jnp.float32
    )
    beta_in = beta_logit.astype(jnp.float32).transpose(0, 2, 1)
    mapped = jax.vmap(partial(decay_forward, block_len=block_len))

    def forward_all(query_in, key_in, value_in, decay_in, beta_all, state_all):
        return mapped(query_in, key_in, value_in, decay_in, beta_all, state_all, keep_mask)

    outputs, pullback = jax.vjp(
        forward_all,
        split_heads(query_rows),
        split_heads(key_rows),
        split_heads(value_rows),
        split_heads(log_decay),
        beta_in,
        states,
    )
    cotangent = split_heads(out_grad) * keep_mask[:, None, :, None]
    grad_q, grad_k, grad_v, grad_g, grad_b, grad_s = pullback(cotangent)
    gradients = (
        join_heads(grad_q),
        join_heads(grad_k),
        join_heads(grad_v),
        join_heads(grad_g),
        grad_b.transpose(0, 2, 1).astype(jnp.bfloat16),
    )
    return (gradients, grad_s)


def per_device(
    query_rows,
    key_rows,
    value_rows,
    log_decay,
    beta_logit,
    out_grad,
    fork_state,
    branch_prompt,
    valid_len,
):
    upper_limit = lax.Precision.HIGHEST
    local_count = query_rows.shape[0]
    head_count = lax.axis_size("head")
    group_size = local_count * head_count
    group_first = lax.axis_index("grp") * group_size
    prompt_count = fork_state.shape[0]
    prompt_ids = jnp.arange(prompt_count, dtype=jnp.int32)
    window_len = query_rows.shape[1]
    group_prompt = lax.dynamic_slice_in_dim(branch_prompt, group_first, group_size)
    group_onehot = (group_prompt[:, None] == prompt_ids[None, :]).astype(jnp.float32)
    group_states = jnp.einsum("bp,phij->bhij", group_onehot, fork_state, precision=upper_limit)
    arrived = (
        lax.all_to_all(query_rows, "head", split_axis=2, concat_axis=0, tiled=True),
        lax.all_to_all(key_rows, "head", split_axis=2, concat_axis=0, tiled=True),
        lax.all_to_all(value_rows, "head", split_axis=2, concat_axis=0, tiled=True),
        lax.all_to_all(log_decay, "head", split_axis=2, concat_axis=0, tiled=True),
        lax.all_to_all(out_grad, "head", split_axis=2, concat_axis=0, tiled=True),
        lax.all_to_all(beta_logit, "head", split_axis=2, concat_axis=0, tiled=True),
    )
    group_len = lax.dynamic_slice_in_dim(valid_len, group_first, group_size)
    gradients, state_grad = branch_backward(
        arrived[0],
        arrived[1],
        arrived[2],
        arrived[3],
        arrived[4],
        arrived[5],
        group_states,
        group_len,
        window_len,
    )
    prompt_grad = jnp.einsum("bp,bhij->phij", group_onehot, state_grad, precision=upper_limit)
    results = (
        lax.all_to_all(gradients[0], "head", split_axis=0, concat_axis=2, tiled=True),
        lax.all_to_all(gradients[1], "head", split_axis=0, concat_axis=2, tiled=True),
        lax.all_to_all(gradients[2], "head", split_axis=0, concat_axis=2, tiled=True),
        lax.all_to_all(gradients[3], "head", split_axis=0, concat_axis=2, tiled=True),
        lax.all_to_all(gradients[4], "head", split_axis=0, concat_axis=2, tiled=True),
    )
    grad_fork = lax.psum(prompt_grad, "grp")
    return (results[0], results[1], results[2], results[3], results[4], grad_fork)


def solution(mesh):
    return jax.shard_map(
        per_device,
        mesh=mesh,
        in_specs=(
            P(("grp", "head"), None, None),
            P(("grp", "head"), None, None),
            P(("grp", "head"), None, None),
            P(("grp", "head"), None, None),
            P(("grp", "head"), None, None),
            P(("grp", "head"), None, None),
            P(None, "head", None, None),
            P(),
            P(),
        ),
        out_specs=(
            P(("grp", "head"), None, None),
            P(("grp", "head"), None, None),
            P(("grp", "head"), None, None),
            P(("grp", "head"), None, None),
            P(("grp", "head"), None, None),
            P(None, "head", None, None),
        ),
        check_vma=False,
    )
```

profile of v0, /device:TPU:1, one launch (start us, length us, event | category | flops | bytes accessed | tf_op | source)
XLA Modules:
  0.0 567.8 jit_solution(9979392489376102869)
XLA Ops:
  8.5 7.6 %all-to-all-start.3 = ((bf16[1,128,16]{1,0,2:T(2,128)(2,1)}), bf16[1,128,16]{1,0,2:T(2,128)(2,1)S(1)}, u32[]{:S(2)}, u32[]{:S(2)}) async-start(bf16[1,128,16]{1,0,2:T(2,128)(2,1)} %copy.205), calls=%async_computation.3 | async-start | bytes 16384 | tf_op jit(solution)/shard_map/all_to_all | solution.py:131
  19.8 11.5 %reduce.13 = bf16[2048,128]{1,0:T(8,128)(2,1)S(1)} reduce(bf16[2048,1,128]{2,1,0:T(2,128)(2,1)S(1)} %bitcast.201, bf16[]{:T(256)} %broadcast.315), dimensions={1}, to_apply=%bitcast.156.reduce_sub_computation | reduce | bytes 1048578
  32.3 7.0 %all-to-all-start.5 = ((bf16[16,2,8192]{2,1,0:T(2,128)(2,1)}), bf16[16,2,8192]{2,1,0:T(2,128)(2,1)S(1)}, u32[]{:S(2)}, u32[]{:S(2)}) async-start(bf16[16,2,8192]{2,1,0:T(2,128)(2,1)} %reshape.506), calls=%async_computation.5 | async-start | bytes 1048576 | tf_op jit(solution)/shard_map/all_to_all | solution.py:126
  40.0 11.5 %reduce.10 = bf16[2048,128]{1,0:T(8,128)(2,1)S(1)} reduce(bf16[2048,1,128]{2,1,0:T(2,128)(2,1)S(1)} %bitcast.205, bf16[]{:T(256)} %broadcast.315), dimensions={1}, to_apply=%bitcast.158.reduce_sub_computation | reduce | bytes 1048578
  53.4 11.5 %reduce.11 = bf16[2048,128]{1,0:T(8,128)(2,1)S(1)} reduce(bf16[2048,1,128]{2,1,0:T(2,128)(2,1)S(1)} %bitcast.206, bf16[]{:T(256)} %broadcast.315), dimensions={1}, to_apply=%bitcast.162.reduce_sub_computation | reduce | bytes 1048578
  66.8 11.9 %reduce.12 = bf16[2048,128]{1,0:T(8,128)(2,1)S(1)} reduce(bf16[2048,1,128]{2,1,0:T(2,128)(2,1)S(1)} %bitcast.207, bf16[]{:T(256)} %broadcast.315), dimensions={1}, to_apply=%bitcast.160.reduce_sub_computation | reduce | bytes 1048578
  80.5 11.5 %reduce.14 = bf16[2048,128]{1,0:T(8,128)(2,1)S(1)} reduce(bf16[2048,1,128]{2,1,0:T(2,128)(2,1)S(1)} %bitcast.202, bf16[]{:T(256)} %broadcast.315), dimensions={1}, to_apply=%bitcast.164.reduce_sub_computation | reduce | bytes 1048578
  94.9 6.7 %all-to-all-start.1 = ((bf16[16,2,8192]{2,1,0:T(2,128)(2,1)}), bf16[16,2,8192]{2,1,0:T(2,128)(2,1)S(1)}, u32[]{:S(2)}, u32[]{:S(2)}) async-start(bf16[16,2,8192]{2,1,0:T(2,128)(2,1)} %reshape.508), calls=%async_computation.1 | async-start | bytes 1048576 | tf_op jit(solution)/shard_map/all_to_all | solution.py:127
  103.4 7.9 %all-to-all-done.1 = bf16[16,2,8192]{2,1,0:T(2,128)(2,1)S(1)} async-done(((bf16[16,2,8192]{2,1,0:T(2,128)(2,1)}), bf16[16,2,8192]{2,1,0:T(2,128)(2,1)S(1)}, u32[]{:S(2)}, u32[]{:S(2)}) %all-to-all-start.1) | async-done | bytes 524320 | tf_op jit(solution)/shard_map/all_to_all | solution.py:127
  111.3 4.4 all-to-all-start.2
  117.6 7.1 %all-to-all-done.2 = bf16[16,2,8192]{2,1,0:T(2,128)(2,1)} async-done(((bf16[16,2,8192]{2,1,0:T(2,128)(2,1)}), bf16[16,2,8192]{2,1,0:T(2,128)(2,1)}, u32[]{:S(2)}, u32[]{:S(2)}) %all-to-all-start.2) | async-done | bytes 524320 | tf_op jit(solution)/shard_map/all_to_all | solution.py:129
  124.7 4.2 all-to-all-start
  143.5 157.8 %custom-call.7 = f32[16,1,128,128]{2,3,1,0:T(8,128)} custom-call(f32[16,1,128,128]{3,2,1,0:T(8,128)S(1)} %add_bitcast_fusion), custom_call_target="InvertDiagBlocksLowerTriangular" | custom-call | tf_op jit(solution)/shard_map/jvp(vmap(jit(_solve_triangular)))/triangular_solve | solution.py:42
  301.3 6.6 %all-to-all-start.4 = ((bf16[16,2,8192]{2,1,0:T(2,128)(2,1)}), bf16[16,2,8192]{2,1,0:T(2,128)(2,1)}, u32[]{:S(2)}, u32[]{:S(2)}) async-start(bf16[16,2,8192]{2,1,0:T(2,128)(2,1)} %reshape.514), calls=%async_computation.4 | async-start | bytes 1048576 | tf_op jit(solution)/shard_map/all_to_all | solution.py:128
  317.0 3.9 reshape.515
  325.2 3.4 convolution_multiply_fusion
  334.8 3.5 multiply_reduce_fusion.1
  345.0 3.3 multiply_reduce_fusion
  349.0 6.4 %all-to-all-start.10 = ((bf16[16,128,1]{1,2,0:T(2,128)(2,1)}), bf16[16,128,1]{1,2,0:T(2,128)(2,1)S(1)}, u32[]{:S(2)}, u32[]{:S(2)}) async-start(bf16[16,128,1]{1,2,0:T(2,128)(2,1)} %copy.235), calls=%async_computation.10 | async-start | bytes 16384 | tf_op jit(solution)/shard_map/all_to_all | solution.py:151
  355.5 4.2 fusion.31
  365.2 4.3 multiply_reduce_fusion.2
  372.2 3.5 multiply_convert_fusion
  376.6 6.7 %all-to-all-start.9 = ((bf16[16,128,128]{2,1,0:T(8,128)(2,1)}), bf16[16,128,128]{2,1,0:T(8,128)(2,1)}, u32[]{:S(2)}, u32[]{:S(2)}) async-start(bf16[16,128,128]{2,1,0:T(8,128)(2,1)} %copy.231), calls=%async_computation.9 | async-start | bytes 1048576 | tf_op jit(solution)/shard_map/all_to_all | solution.py:150
  383.3 4.0 fusion.4
  387.3 5.0 all-to-all-done.9
  392.4 13.4 %all_to_all.144 = bf16[16,128,128]{1,2,0:T(8,128)(2,1)} all-to-all(bf16[16,128,128]{1,2,0:T(8,128)(2,1)} %get-tuple-element.45), channel_id=1, replica_groups=mesh['grp'=16,'head'=16] {'head'}, dimensions={0} | all-to-all | bytes 1048576 | tf_op jit(solution)/shard_map/all_to_all | solution.py:147
  405.7 4.5 all-to-all-start.7
  410.2 3.3 fusion.8
  413.5 5.7 %all-to-all-done.7 = bf16[16,128,128]{1,2,0:T(8,128)(2,1)} async-done(((bf16[16,128,128]{1,2,0:T(8,128)(2,1)}), bf16[16,128,128]{1,2,0:T(8,128)(2,1)}, u32[]{:S(2)}, u32[]{:S(2)}) %all-to-all-start.7) | async-done | bytes 524320 | tf_op jit(solution)/shard_map/all_to_all | solution.py:148
  419.2 4.2 all-to-all-start.8
  423.5 3.4 fusion
  429.3 121.8 %all-reduce.2.cloned.1.call-done = f32[8,1,128,128]{3,0,2,1:T(8,128)} async-done(((f32[8,1,128,128]{3,0,2,1:T(8,128)}), f32[8,1,128,128]{3,0,2,1:T(8,128)}) %all-reduce.2.cloned.1.call-update) | async-done | bytes 524304 | tf_op jit(solution)/shard_map/psum | solution.py:153
  (136 shorter events, 81.0 us)
Async XLA Ops:
  7.2 85.9 %copy-start = (f32[8,1,128,128]{3,2,1,0:T(8,128)S(1)}, f32[8,1,128,128]{3,2,1,0:T(8,128)}, u32[]{:S(2)}) copy-start(f32[8,1,128,128]{3,2,1,0:T(8,128)} %param.17) | copy-start | bytes 1572868
  8.5 23.7 %all-to-all-start.3 = ((bf16[1,128,16]{1,0,2:T(2,128)(2,1)}), bf16[1,128,16]{1,0,2:T(2,128)(2,1)S(1)}, u32[]{:S(2)}, u32[]{:S(2)}) async-start(bf16[1,128,16]{1,0,2:T(2,128)(2,1)} %copy.205), calls=%async_computation.3 | async-start | bytes 16384 | tf_op jit(solution)/shard_map/all_to_all | solution.py:131
  32.2 7.0 %copy-start.24 = (bf16[1,128,2048]{2,1,0:T(8,128)(2,1)S(1)}, bf16[1,128,2048]{2,1,0:T(8,128)(2,1)}, u32[]{:S(2)}) copy-start(bf16[1,128,2048]{2,1,0:T(8,128)(2,1)} %param.12) | copy-start | bytes 1572868
  32.3 62.6 %all-to-all-start.5 = ((bf16[16,2,8192]{2,1,0:T(2,128)(2,1)}), bf16[16,2,8192]{2,1,0:T(2,128)(2,1)S(1)}, u32[]{:S(2)}, u32[]{:S(2)}) async-start(bf16[16,2,8192]{2,1,0:T(2,128)(2,1)} %reshape.506), calls=%async_computation.5 | async-start | bytes 1048576 | tf_op jit(solution)/shard_map/all_to_all | solution.py:126
  94.9 16.4 %all-to-all-start.1 = ((bf16[16,2,8192]{2,1,0:T(2,128)(2,1)}), bf16[16,2,8192]{2,1,0:T(2,128)(2,1)S(1)}, u32[]{:S(2)}, u32[]{:S(2)}) async-start(bf16[16,2,8192]{2,1,0:T(2,128)(2,1)} %reshape.508), calls=%async_computation.1 | async-start | bytes 1048576 | tf_op jit(solution)/shard_map/all_to_all | solution.py:127
  111.3 13.4 %all-to-all-start.2 = ((bf16[16,2,8192]{2,1,0:T(2,128)(2,1)}), bf16[16,2,8192]{2,1,0:T(2,128)(2,1)}, u32[]{:S(2)}, u32[]{:S(2)}) async-start(bf16[16,2,8192]{2,1,0:T(2,128)(2,1)} %reshape.512), calls=%async_computation.2 | async-start | bytes 1048576 | tf_op jit(solution)/shard_map/all_to_all | solution.py:129
  124.7 176.6 %all-to-all-start = ((bf16[16,2,8192]{2,1,0:T(2,128)(2,1)}), bf16[16,2,8192]{2,1,0:T(2,128)(2,1)}, u32[]{:S(2)}, u32[]{:S(2)}) async-start(bf16[16,2,8192]{2,1,0:T(2,128)(2,1)} %reshape.510), calls=%async_computation | async-start | bytes 1048576 | tf_op jit(solution)/shard_map/all_to_all | solution.py:130
  137.7 1.5 copy-start.11
  139.2 2.9 copy-start.4
  301.3 15.7 %all-to-all-start.4 = ((bf16[16,2,8192]{2,1,0:T(2,128)(2,1)}), bf16[16,2,8192]{2,1,0:T(2,128)(2,1)}, u32[]{:S(2)}, u32[]{:S(2)}) async-start(bf16[16,2,8192]{2,1,0:T(2,128)(2,1)} %reshape.514), calls=%async_computation.4 | async-start | bytes 1048576 | tf_op jit(solution)/shard_map/all_to_all | solution.py:128
  328.6 1.2 copy-start.5
  328.6 1.5 copy-start.10
  328.6 1.8 copy-start.22
  330.5 2.2 copy-start.19
  342.6 2.4 copy-start.17
  349.0 27.6 %all-to-all-start.10 = ((bf16[16,128,1]{1,2,0:T(2,128)(2,1)}), bf16[16,128,1]{1,2,0:T(2,128)(2,1)S(1)}, u32[]{:S(2)}, u32[]{:S(2)}) async-start(bf16[16,128,1]{1,2,0:T(2,128)(2,1)} %copy.235), calls=%async_computation.10 | async-start | bytes 16384 | tf_op jit(solution)/shard_map/all_to_all | solution.py:151
  355.4 4.2 copy-start.8
  355.4 4.2 copy-start.15
  359.7 1.2 copy-start.3
  359.7 1.5 copy-start.21
  361.2 2.3 copy-start.6
  361.2 2.3 copy-start.20
  363.6 1.4 copy-start.13
  363.6 1.6 copy-start.12
  364.9 4.5 copy-start.14
  376.6 15.8 %all-to-all-start.9 = ((bf16[16,128,128]{2,1,0:T(8,128)(2,1)}), bf16[16,128,128]{2,1,0:T(8,128)(2,1)}, u32[]{:S(2)}, u32[]{:S(2)}) async-start(bf16[16,128,128]{2,1,0:T(8,128)(2,1)} %copy.231), calls=%async_computation.9 | async-start | bytes 1048576 | tf_op jit(solution)/shard_map/all_to_all | solution.py:150
  392.4 17.8 %copy-start.9 = (f32[16,1,128,128]{2,3,0,1:T(8,128)S(1)}, f32[16,1,128,128]{2,3,0,1:T(8,128)}, u32[]{:S(2)}) copy-start(f32[16,1,128,128]{2,3,0,1:T(8,128)} %get-tuple-element.46) | copy-start | bytes 3145732
  405.7 13.5 %all-to-all-start.7 = ((bf16[16,128,128]{1,2,0:T(8,128)(2,1)}), bf16[16,128,128]{1,2,0:T(8,128)(2,1)}, u32[]{:S(2)}, u32[]{:S(2)}) async-start(bf16[16,128,128]{1,2,0:T(8,128)(2,1)} %get-tuple-element.44), calls=%async_computation.7 | async-start | bytes 1048576 | tf_op jit(solution)/shard_map/all_to_all | solution.py:148
  410.2 13.3 %copy-start.18 = (f32[16,128,128]{2,1,0:T(8,128)S(1)}, f32[16,128,128]{2,1,0:T(8,128)}, u32[]{:S(2)}) copy-start(f32[16,128,128]{2,1,0:T(8,128)} %get-tuple-element.50) | copy-start | bytes 3145732
  413.5 10.0 %copy-start.7 = (f32[16,1,128,128]{2,3,0,1:T(8,128)S(1)}, f32[16,1,128,128]{2,3,0,1:T(8,128)}, u32[]{:S(2)}) copy-start(f32[16,1,128,128]{2,3,0,1:T(8,128)} %copy-done.4) | copy-start | bytes 3145732
  419.2 139.2 %all-to-all-start.8 = ((bf16[16,128,128]{2,1,0:T(8,128)(2,1)}), bf16[16,128,128]{2,1,0:T(8,128)(2,1)}, u32[]{:S(2)}, u32[]{:S(2)}) async-start(bf16[16,128,128]{2,1,0:T(8,128)(2,1)} %get-tuple-element.43), calls=%async_computation.8 | async-start | bytes 1048576 | tf_op jit(solution)/shard_map/all_to_all | solution.py:149
  423.4 127.6 %all-reduce.2.cloned.1.call-start = ((), (), s32[]{:S(2)}) async-start(), calls=%async_computation.11 | async-start | bytes 1048576 | tf_op jit(solution)/shard_map/psum | solution.py:153
  (9 other events, 8.9 us)
Sparse Core Ops, SparseCore 0:
  428.8 122.1 all-reduce.1
where the time goes:
time: 575 us; the launch traced here: 568 us
  other arithmetic  234 us (41%)
  waiting for transfers between devices  148 us (26%)
  starting transfers between devices  58.5 us (10%)
  local copies, waits for them, and re-layouts  51.7 us (9%)
  matrix products  47.2 us (8%)
  between operations  14.9 us (3%)
  blocking collectives  13.4 us (2%)
    another operation x4, other arithmetic, decay_forward(): jax.scipy.linalg.solve_triangular(identity_block + coupling, target_outpu...  158 us
    psum x1, waiting for transfers between devices, per_device(): grad_fork = lax.psum(prompt_grad, 'grp')  122 us
    unnamed x5, other arithmetic  58.1 us
    unnamed x83, local copies, waits for them, and re-layouts  33.1 us
    all_to_all x1, blocking collectives, per_device(): lax.all_to_all(gradients[0], 'head', split_axis=0, concat_axis=2, tiled=T...  13.4 us
  transfers between devices with their start and end apart: 11, of which 6 were waited for; matrix products, arithmetic and copies ran while one was open for 52% of the time, Pallas kernels for 0%

commit v1 on v0

v1 whole, which is shorter than its diff:
```python
import jax
import jax.numpy as jnp
from jax import lax
from jax.experimental import pallas as pl
from jax.experimental.pallas import tpu as pltpu
from jax.sharding import PartitionSpec as P

F32 = jnp.float32
BF16 = jnp.bfloat16
MESH = pl.DeviceIdType.MESH
D = 128
HALF = 64
HEADS = 16
GROUPS = 16
PROMPTS = 8
HA = 2
HB = 2
SCALE = D**-0.5


def dot(a, b, ca, cb):
    return lax.dot_general(a, b, (((ca,), (cb,)), ((), ())), preferred_element_type=F32)


def split(x):
    hi = x.astype(BF16)
    return hi, (x - hi.astype(F32)).astype(BF16)


def cat(parts, axis):
    return jnp.concatenate(parts, axis=axis)


def mm3(a, b, ca, cb):
    return dot(cat([a[0], a[0], a[1]], ca), cat([b[0], b[1], b[0]], cb), ca, cb)


def mm2(a, b, ca, cb):
    return dot(cat([a, a], ca), cat([b[0], b[1]], cb), ca, cb)


def kernel(
    prompt_ref, len_ref, q_ref, k_ref, v_ref, g_ref, beta_ref, do_ref, fork_ref,
    gq_ref, gk_ref, gv_ref, gg_ref, gb_ref, gf_ref,
    s_send, s_recv, ds_send, ds_recv, acc, pair_recv, comb, rs_recv,
    u_s, w_s, decay_s, qf_s, kf_s, ke_s, kt_s, tt_s, mask_s, tri_s, beta_s, betat_s, gb_s,
    s_ssem, s_rsem, d_ssem, d_rsem, p_ssem, p_rsem, r_ssem, r_rsem, a_ssem, a_rsem, f_ssem, f_rsem,
):
    grp = lax.axis_index("grp")
    me = lax.axis_index("head")
    core = lax.rem(grp, 2)
    zed = grp // 2
    base = grp * HEADS

    def head_peer(o):
        return (grp, lax.rem(me + o, HEADS))

    def z_peer(o):
        return (lax.rem(zed + o, PROMPTS) * 2 + core, me)

    partner = (zed * 2 + 1 - core, me)

    barrier = pltpu.get_barrier_semaphore()

    def greet_head(o, c):
        pl.semaphore_signal(barrier, inc=1, device_id=head_peer(o), device_id_type=MESH)
        return c

    def greet_z(o, c):
        pl.semaphore_signal(barrier, inc=1, device_id=z_peer(o), device_id_type=MESH)
        return c

    lax.fori_loop(1, HEADS, greet_head, 0)
    lax.fori_loop(1, PROMPTS, greet_z, 0)
    pl.semaphore_signal(barrier, inc=1, device_id=partner, device_id_type=MESH)

    def pack_state(o, c):
        s_send[o] = fork_ref[prompt_ref[base + lax.rem(me + o, HEADS)], 0]
        return c

    s_recv[0] = fork_ref[prompt_ref[base + me], 0]
    lax.fori_loop(1, HEADS, pack_state, 0)

    row = lax.broadcasted_iota(jnp.int32, (D, D), 0)
    col = lax.broadcasted_iota(jnp.int32, (D, D), 1)
    xor = jnp.where(row < col, jnp.bitwise_xor(row, col), 0)
    for level in range(7):
        m = 1 << level
        mask_s[level] = jnp.where((xor >= m) & (xor < 2 * m), 1.0, 0.0).astype(BF16)
    lower = jnp.where(col <= row, 1.0, 0.0) - jnp.where(col < HALF, 1.0, 0.0)
    tri_s[0] = lower.astype(BF16)
    tri_s[1] = jnp.where(col >= row, 1.0, 0.0).astype(BF16)
    valid = len_ref[base + me]
    keep_col = jnp.where(lax.broadcasted_iota(jnp.int32, (D, 1), 0) < valid, 1.0, 0.0)
    beta_all = jax.nn.sigmoid(beta_ref[0].astype(F32))
    beta_pad = cat([beta_all, jnp.zeros((D, D - HEADS), F32)], 1) * keep_col
    beta_s[...] = beta_pad
    betat_s[...] = beta_pad.T
    gb_s[...] = jnp.zeros((D, D), F32)

    pl.semaphore_wait(barrier, HEADS - 1 + PROMPTS - 1 + 1)

    def state_copy(o):
        return pltpu.make_async_remote_copy(
            src_ref=s_send.at[o], dst_ref=s_recv.at[o], send_sem=s_ssem.at[o], recv_sem=s_rsem.at[o],
            device_id=head_peer(o), device_id_type=MESH)

    def send_state(o, c):
        state_copy(o).start()
        return c

    lax.fori_loop(1, HEADS, send_state, 0)

    def head_lanes(h):
        return pl.ds(pl.multiple_of(h * D, D), D)

    def beta_column(h):
        return jnp.sum(jnp.where(col == h, beta_s[...], 0.0), axis=1, keepdims=True)

    def keep_rows():
        return lax.broadcasted_iota(jnp.int32, (D, 1), 0) < valid

    def slot_of(h):
        return lax.rem(h - me + HEADS, HEADS)

    def grad_copy(h):
        o = slot_of(h)
        return pltpu.make_async_remote_copy(
            src_ref=ds_send.at[o], dst_ref=ds_recv.at[o], send_sem=d_ssem.at[o], recv_sem=d_rsem.at[o],
            device_id=(grp, h), device_id_type=MESH)

    def phase_a(h):
        lanes = head_lanes(h)
        keep = keep_rows()
        q = q_ref[0, :, lanes].astype(F32)
        k = k_ref[0, :, lanes].astype(F32)
        uq = q * (lax.rsqrt(jnp.sum(q * q, axis=1, keepdims=True) + 1e-6) * SCALE)
        uk = k * lax.rsqrt(jnp.sum(k * k, axis=1, keepdims=True) + 1e-6)
        decay = jnp.where(keep, g_ref[0, :, lanes].astype(F32), 0.0)
        cum = dot(tri_s[0], decay.astype(BF16), 1, 0)
        ee = jnp.exp(decay[0:1] - cum[0:1])
        eg = jnp.exp(cum)
        es = jnp.exp(-cum)
        qf, kf = uq * eg, uk * eg
        qfs, kfs, kes = split(qf), split(kf), split(uk * es)
        qts, kts = split(qf * ee), split(kf * ee)
        u_s[h, 0], u_s[h, 1] = uq, uk
        decay_s[h, 0], decay_s[h, 1] = eg, es
        for i in range(2):
            qf_s[h, i], kf_s[h, i], ke_s[h, i], kt_s[h, i] = qfs[i], kfs[i], kes[i], kts[i]
        both = tuple(cat([kfs[i], qfs[i]], 0) for i in range(2))
        scores = mm3(kes, both, 1, 1)
        beta_row = betat_s[pl.ds(h, 1), :]
        coupling = split(jnp.where(row < col, scores[:, :D] * beta_row, 0.0))
        attend = split(jnp.where(row <= col, scores[:, D:], 0.0))
        do = jnp.where(keep, do_ref[0, :, lanes].astype(F32), 0.0).astype(BF16)
        du = split(dot(cat([attend[0], attend[1]], 1), cat([do, do], 0), 1, 0))
        eye = jnp.where(row == col, 1.0, 0.0)
        inv = eye - (coupling[0] * mask_s[0]).astype(F32) - (coupling[1] * mask_s[0]).astype(F32)
        for level in range(1, 7):
            mask = mask_s[level]
            inv_p = split(inv)
            step = split(mm3((coupling[0] * mask, coupling[1] * mask), inv_p, 1, 0))
            inv = inv - mm3(inv_p, step, 1, 0)
        inv_p = split(inv)
        tt_s[h, 0], tt_s[h, 1] = inv_p
        w = mm3(inv_p, du, 1, 0)
        w_s[h] = w
        nbw = split(-(beta_column(h) * w))
        ds = dot(
            cat([qts[0], qts[1], kts[0], kts[0], kts[1]], 0),
            cat([do, do, nbw[0], nbw[1], nbw[0]], 0), 0, 0)
        o = slot_of(h)
        ds_send[o] = ds

        @pl.when(o == 0)
        def _():
            ds_recv[0] = ds

    def phase_b(h):
        lanes = head_lanes(h)
        keep = keep_rows()
        q = q_ref[0, :, lanes].astype(F32)
        k = k_ref[0, :, lanes].astype(F32)
        rq = lax.rsqrt(jnp.sum(q * q, axis=1, keepdims=True) + 1e-6)
        rk = lax.rsqrt(jnp.sum(k * k, axis=1, keepdims=True) + 1e-6)
        uq, uk = u_s[h, 0], u_s[h, 1]
        eg, es = decay_s[h, 0], decay_s[h, 1]
        pair = lambda ref: (ref[h, 0], ref[h, 1])
        qfs, kfs, kes, kts, tts = pair(qf_s), pair(kf_s), pair(ke_s), pair(kt_s), pair(tt_s)
        w = w_s[h]
        beta = beta_column(h)
        nbw_f = -(beta * w)
        nbw = split(nbw_f)
        do = jnp.where(keep, do_ref[0, :, lanes].astype(F32), 0.0).astype(BF16)
        ss = split(s_recv[lax.rem(me - h + HEADS, HEADS)])
        v = v_ref[0, :, lanes].astype(F32)
        target = split(beta * (v - mm3(kts, ss, 1, 0)))
        u = mm3(tts, target, 0, 0)
        us = split(u)
        dp = split(jnp.where(row >= col, mm2(do, us, 1, 1), 0.0))
        dn = split(jnp.where(row > col, mm3(nbw, us, 1, 1), 0.0))
        decay0 = jnp.where(keep, g_ref[0, :, lanes].astype(F32), 0.0)[0:1]
        cum0 = dot(tri_s[0, 0:16], jnp.where(keep, g_ref[0, :, lanes].astype(F32), 0.0).astype(BF16), 1, 0)[0:1]
        ee = jnp.exp(decay0 - cum0)
        dqf = mm2(do, ss, 1, 1) * ee + mm3(dp, kes, 1, 0)
        dkf = mm3(nbw, ss, 1, 1) * ee + mm3(dn, kes, 1, 0)
        dke = dot(
            cat([dn[0], dn[0], dn[1], dp[0], dp[0], dp[1]], 0),
            cat([kfs[0], kfs[1], kfs[0], qfs[0], qfs[1], qfs[0]], 0), 0, 0)
        dqg, dkg, dks = dqf * eg, dkf * eg, dke * es
        dc = split(dqg * uq + dkg * uk - dks * uk)
        dg = mm2(tri_s[1], dc, 1, 0)
        gg_ref[0, :, lanes] = jnp.where(keep, dg, 0.0).astype(BF16)
        duk = dkg + dks
        gq = rq * (SCALE * dqg - uq * (jnp.sum(uq * dqg, axis=1, keepdims=True) * (1.0 / SCALE)))
        gk = rk * (duk - uk * jnp.sum(uk * duk, axis=1, keepdims=True))
        gq_ref[0, :, lanes] = gq.astype(BF16)
        gk_ref[0, :, lanes] = gk.astype(BF16)
        gv_ref[0, :, lanes] = (-nbw_f).astype(BF16)
        db = jnp.where(keep, (1.0 - beta) * jnp.sum(w * u, axis=1, keepdims=True), 0.0)
        gb_s[...] = jnp.where(col == h, db, gb_s[...])

    def loop_a(i, c):
        first = lax.rem(me // HA + i, HEADS // HA) * HA
        for n in range(HA):
            phase_a(first + n)
        for n in range(HA):
            h = first + n

            @pl.when(h != me)
            def _():
                grad_copy(h).start()

        return c

    lax.fori_loop(0, HEADS // HA, loop_a, 0)

    def wait_state(o, c):
        state_copy(o).wait()
        return c

    lax.fori_loop(1, HEADS, wait_state, 0)

    def pair_copy():
        return pltpu.make_async_remote_copy(
            src_ref=acc.at[1 - core], dst_ref=pair_recv, send_sem=p_ssem, recv_sem=p_rsem,
            device_id=partner, device_id_type=MESH)

    def rs_copy(o):
        return pltpu.make_async_remote_copy(
            src_ref=comb.at[lax.rem(zed + o, PROMPTS)], dst_ref=rs_recv.at[o],
            send_sem=r_ssem.at[o], recv_sem=r_rsem.at[o], device_id=z_peer(o), device_id_type=MESH)

    def piece(p, c):
        return gf_ref.at[p, 0, pl.ds(pl.multiple_of(c * HALF, HALF), HALF)]

    def ag_copy(o):
        return pltpu.make_async_remote_copy(
            src_ref=piece(zed, core), dst_ref=piece(zed, core),
            send_sem=a_ssem.at[o], recv_sem=a_rsem.at[o], device_id=z_peer(o), device_id_type=MESH)

    def hand_copy(o):
        p = lax.rem(zed - o + PROMPTS, PROMPTS)
        return pltpu.make_async_remote_copy(
            src_ref=piece(p, core), dst_ref=piece(p, core),
            send_sem=f_ssem.at[o], recv_sem=f_rsem.at[o], device_id=partner, device_id_type=MESH)

    def stage_sum():
        def wait_grad(o, c):
            copy = pltpu.make_async_remote_copy(
                src_ref=ds_send.at[o], dst_ref=ds_recv.at[o], send_sem=d_ssem.at[o], recv_sem=d_rsem.at[o],
                device_id=head_peer(o), device_id_type=MESH)
            copy.wait()
            return c

        lax.fori_loop(1, HEADS, wait_grad, 0)

        def sum_rows(r, c):
            half = r // 8
            rows = pl.ds(pl.multiple_of(r * 8, 8), 8)
            out_rows = pl.ds(pl.multiple_of(lax.rem(r, 8) * 8, 8), 8)
            totals = [jnp.zeros((8, D), F32)] * PROMPTS
            for o in range(HEADS):
                part = ds_recv[o, rows, :]
                source = prompt_ref[base + lax.rem(me - o + HEADS, HEADS)]
                for p in range(PROMPTS):
                    totals[p] = totals[p] + jnp.where(source == p, 1.0, 0.0) * part
            for p in range(PROMPTS):
                acc[half, p, out_rows, :] = totals[p]
            return c

        lax.fori_loop(0, 16, sum_rows, 0)
        pair_copy().start()

    def stage_scatter():
        pair_copy().wait()
        comb[...] = acc[core] + pair_recv[...]
        lax.fori_loop(1, PROMPTS, lambda o, c: (rs_copy(o).start(), c)[1], 0)

    def stage_gather():
        lax.fori_loop(1, PROMPTS, lambda o, c: (rs_copy(o).wait(), c)[1], 0)
        total = comb[zed]
        for o in range(1, PROMPTS):
            total = total + rs_recv[o]
        gf_ref[zed, 0, pl.ds(pl.multiple_of(core * HALF, HALF), HALF)] = total
        lax.fori_loop(1, PROMPTS, lambda o, c: (ag_copy(o).start(), c)[1], 0)
        hand_copy(0).start()

    def stage_hand():
        def forward(o, c):
            ag_copy(o).wait()
            hand_copy(o).start()
            return c

        lax.fori_loop(1, PROMPTS, forward, 0)

    steps = HEADS // HB
    stages = {1: stage_sum, 2: stage_scatter, 4: stage_gather, 6: stage_hand}

    def loop_b(i, c):
        for at, stage in stages.items():
            pl.when(i == at)(stage)
        for n in range(HB):
            phase_b(i * HB + n)
        return c

    lax.fori_loop(0, steps, loop_b, 0)
    gb_ref[0] = gb_s[:, :HEADS].astype(BF16)
    lax.fori_loop(0, PROMPTS, lambda o, c: (hand_copy(o).wait(), c)[1], 0)


def per_device(query_rows, key_rows, value_rows, log_decay, beta_logit, out_grad, fork_state, branch_prompt, valid_len):
    vmem = pl.BlockSpec(memory_space=pltpu.VMEM)
    smem = pl.BlockSpec(memory_space=pltpu.SMEM)
    rows = jax.ShapeDtypeStruct(query_rows.shape, BF16)
    dma = pltpu.SemaphoreType.DMA
    pairs = pltpu.VMEM((HEADS, 2, D, D), BF16)
    return pl.pallas_call(
        kernel,
        out_shape=(
            rows, rows, rows, rows,
            jax.ShapeDtypeStruct(beta_logit.shape, BF16),
            jax.ShapeDtypeStruct(fork_state.shape, F32),
        ),
        in_specs=[smem, smem] + [vmem] * 7,
        out_specs=(vmem,) * 6,
        scratch_shapes=[
            pltpu.VMEM((HEADS, D, D), F32),
            pltpu.VMEM((HEADS, D, D), F32),
            pltpu.VMEM((HEADS, D, D), F32),
            pltpu.VMEM((HEADS, D, D), F32),
            pltpu.VMEM((2, PROMPTS, HALF, D), F32),
            pltpu.VMEM((PROMPTS, HALF, D), F32),
            pltpu.VMEM((PROMPTS, HALF, D), F32),
            pltpu.VMEM((PROMPTS, HALF, D), F32),
            pltpu.VMEM((HEADS, 2, D, D), F32),
            pltpu.VMEM((HEADS, D, D), F32),
            pltpu.VMEM((HEADS, 2, D, D), F32),
            pairs, pairs, pairs, pairs, pairs,
            pltpu.VMEM((7, D, D), BF16),
            pltpu.VMEM((2, D, D), BF16),
            pltpu.VMEM((D, D), F32),
            pltpu.VMEM((D, D), F32),
            pltpu.VMEM((D, D), F32),
            dma((HEADS,)), dma((HEADS,)),
            dma((HEADS,)), dma((HEADS,)),
            dma(()), dma(()),
            dma((PROMPTS,)), dma((PROMPTS,)),
            dma((PROMPTS,)), dma((PROMPTS,)),
            dma((PROMPTS,)), dma((PROMPTS,)),
        ],
        compiler_params=pltpu.CompilerParams(collective_id=0, has_side_effects=True),
        name="delta_backward",
    )(branch_prompt, valid_len, query_rows, key_rows, value_rows, log_decay, beta_logit, out_grad, fork_state)


def solution(mesh):
    branch = P(("grp", "head"), None, None)
    state = P(None, "head", None, None)
    return jax.shard_map(
        per_device,
        mesh=mesh,
        in_specs=(branch,) * 6 + (state, P(), P()),
        out_specs=(branch,) * 5 + (state,),
        check_vma=False,
    )
```

time: 575 us -> 94.6 us (0.16); the launches traced: 568 us -> 93.9 us
  other arithmetic: 234 us -> 0 us
  waiting for transfers between devices: 148 us -> 0 us
  Pallas kernels: 0 us -> 84 us
  starting transfers between devices: 58.5 us -> 0 us
  matrix products: 47.2 us -> 0 us
  local copies, waits for them, and re-layouts: 51.7 us -> 9.25 us
  between operations: 14.9 us -> 0.65 us
  blocking collectives: 13.4 us -> 0 us
    another operation x7 -> x0, other arithmetic: 164 us -> none  [the longest x4 158 us: decay_forward(): jax.scipy.linalg.solve_triangular(identity_block + coupling, target_outpu...]
    psum x1 -> x0, waiting for transfers between devices: 122 us -> none  [per_device(): grad_fork = lax.psum(prompt_grad, 'grp')]
    pallas_call x0 -> x1, Pallas kernels: none -> 84 us  [per_device(): pl.pallas_call(kernel, out_shape=(rows, rows, rows, rows, jax.ShapeDtypeS...]
    all_to_all x10 -> x0, starting transfers between devices: 58.4 us -> none  [the longest x1 7.57 us: per_device(): lax.all_to_all(beta_logit, 'head', split_axis=2, concat_axis=0, tiled=True)]
    unnamed x5 -> x0, other arithmetic: 58.1 us -> none
    dot_general x16 -> x0, matrix products: 38.2 us -> none  [the longest x3 9.75 us: decay_forward(): jnp.einsum('led,ldf->lef', key_forward_rows, state_in, precision=upper_li...]
    all_to_all x10 -> x0, waiting for transfers between devices: 26 us -> none  [the longest x1 7.89 us: per_device(): lax.all_to_all(key_rows, 'head', split_axis=2, concat_axis=0, tiled=True)]
    unnamed x83 -> x14, local copies, waits for them, and re-layouts: 33.1 us -> 7.83 us
  transfers between devices with their start and end apart: 11 -> 0, of which waited for: 6 -> 0; matrix products, arithmetic and copies ran while one was open for 52% -> 0% of each run, Pallas kernels for 0% -> 0%
where the time goes in v1:
time: 94.6 us; the launch traced here: 93.9 us
  Pallas kernels  84 us (89%)
  local copies, waits for them, and re-layouts  9.25 us (10%)
    pallas_call x1, Pallas kernels, per_device(): pl.pallas_call(kernel, out_shape=(rows, rows, rows, rows, jax.ShapeDtypeS...  84 us
    unnamed x14, local copies, waits for them, and re-layouts  7.83 us

profile of v1, /device:TPU:1, one launch (start us, length us, event | category | flops | bytes accessed | tf_op | source)
XLA Modules:
  0.0 93.9 jit_solution(17438631269356949351)
XLA Ops:
  0.6 1.4 %copy.15.beta_ref = bf16[1,128,16]{2,1,0:T(8,128)(2,1)} copy(bf16[1,128,16]{1,2,0:T(8,128)(2,1)} %param.13) | data formatting | bytes 8192 | tf_op args[4]
  2.0 84.0 %delta_backward.1 = (bf16[1,128,2048]{2,1,0:T(8,128)(2,1)}, bf16[1,128,2048]{2,1,0:T(8,128)(2,1)}, bf16[1,128,2048]{2,1,0:T(8,128)(2,1)}, bf16[1,128,2048]{2,1,0...) custom-call(s32[256]{0:T(256)} %prompt_ref.1, s32[256]{0:T(256)} %len_ref.1, ...), custom_call_target="tpu_custom_call" | custom-call | tf_op jit(solution)/shard_map/delta_backward/pallas_call | solution.py:339
  86.0 1.4 %copy.16 = bf16[1,128,16]{1,2,0:T(8,128)(2,1)} copy(bf16[1,128,16]{2,1,0:T(8,128)(2,1)} %get-tuple-element.10) | data formatting | bytes 8192 | tf_op jit(solution)/shard_map/delta_backward/pallas_call | solution.py:339
  87.4 0.0 copy-start.3
  87.4 1.9 %copy.22 = bf16[1,128,2048]{2,1,0:T(8,128)(2,1)} copy(bf16[1,128,2048]{2,1,0:T(8,128)(2,1)} %get-tuple-element.18) | data formatting | bytes 1048576
  89.4 0.0 copy-done.3
  89.4 0.0 copy-start.2
  89.4 0.8 copy.23
  90.2 0.4 copy-done.2
  90.6 0.0 copy-start.1
  90.6 0.8 copy.24
  91.4 0.4 copy-done.1
  91.8 0.0 copy-start
  91.8 0.8 copy.25
  92.6 0.4 copy-done
  93.1 0.8 copy.26
Async XLA Ops:
  87.4 1.9 %copy-start.3 = (bf16[1,128,2048]{2,1,0:T(8,128)(2,1)S(1)}, bf16[1,128,2048]{2,1,0:T(8,128)(2,1)}, u32[]{:S(2)}) copy-start(bf16[1,128,2048]{2,1,0:T(8,128)(2,1)} %get-tuple-element.19) | copy-start | bytes 1572868
  89.4 1.2 %copy-start.2 = (bf16[1,128,2048]{2,1,0:T(8,128)(2,1)S(1)}, bf16[1,128,2048]{2,1,0:T(8,128)(2,1)}, u32[]{:S(2)}) copy-start(bf16[1,128,2048]{2,1,0:T(8,128)(2,1)} %get-tuple-element.20) | copy-start | bytes 1572868
  90.6 1.2 %copy-start.1 = (bf16[1,128,2048]{2,1,0:T(8,128)(2,1)S(1)}, bf16[1,128,2048]{2,1,0:T(8,128)(2,1)}, u32[]{:S(2)}) copy-start(bf16[1,128,2048]{2,1,0:T(8,128)(2,1)} %get-tuple-element.21) | copy-start | bytes 1572868
  91.8 1.2 %copy-start = (f32[8,1,128,128]{3,2,1,0:T(8,128)S(1)}, f32[8,1,128,128]{3,2,1,0:T(8,128)}, u32[]{:S(2)}) copy-start(f32[8,1,128,128]{3,2,1,0:T(8,128)} %get-tuple-element.23) | copy-start | bytes 1572868

commit v2 on v1

v2 whole, which is shorter than its diff:
```python
import jax
import jax.numpy as jnp
from jax import lax
from jax.experimental import pallas as pl
from jax.experimental.pallas import tpu as pltpu
from jax.sharding import PartitionSpec as P

F32 = jnp.float32
BF16 = jnp.bfloat16
I16 = jnp.int16
MESH = pl.DeviceIdType.MESH
D = 128
HALF = 64
HEADS = 16
GROUPS = 16
PROMPTS = 8
HA = 8
HB = 4
TAIL = 16
STAGE_SUM = 2
STAGE_SCATTER = 3
STAGE_GATHER = 4
STAGE_HAND = 4
SCALE = D**-0.5


def dot(a, b, ca, cb):
    return lax.dot_general(a, b, (((ca,), (cb,)), ((), ())), preferred_element_type=F32)


def split(x):
    hi = x.astype(BF16)
    return hi, (x - hi.astype(F32)).astype(BF16)


def cat(parts, axis):
    return jnp.concatenate(parts, axis=axis)


def mm3(a, b, ca, cb):
    return dot(cat([a[0], a[0], a[1]], ca), cat([b[0], b[1], b[0]], cb), ca, cb)


def mm2(a, b, ca, cb):
    return dot(cat([a, a], ca), cat([b[0], b[1]], cb), ca, cb)


def encode(x):
    peak = jnp.maximum(jnp.max(jnp.abs(x), axis=0, keepdims=True), 1e-30)
    power = jnp.ceil(jnp.log2(peak))
    code = jnp.clip(jnp.round(x * jnp.exp2(15.0 - power)), -32767.0, 32767.0)
    tail = jnp.broadcast_to(power, (TAIL, x.shape[1]))
    return cat([code, tail], 0).astype(jnp.int32).astype(I16)


def decode(code, tail):
    power = tail[0:1].astype(jnp.int32).astype(F32)
    return code.astype(jnp.int32).astype(F32) * jnp.exp2(power - 15.0)


def kernel(
    prompt_ref, len_ref, q_ref, k_ref, v_ref, g_ref, beta_ref, do_ref, fork_ref,
    gq_ref, gk_ref, gv_ref, gg_ref, gb_ref, gf_ref,
    s_own, s_send, s_recv, ds_send, ds_recv, acc, pair_recv, comb, rs_send, rs_recv, ag,
    u_s, w_s, decay_s, ee_s, qf_s, kf_s, ke_s, kt_s, tt_s, mask_s, tri_s, beta_s, betat_s, gb_s,
    s_ssem, s_rsem, d_ssem, d_rsem, p_ssem, p_rsem, r_ssem, r_rsem, a_ssem, a_rsem, f_ssem, f_rsem,
):
    grp = lax.axis_index("grp")
    me = lax.axis_index("head")
    core = lax.rem(grp, 2)
    zed = grp // 2
    base = grp * HEADS

    def head_peer(o):
        return (grp, lax.rem(me + o, HEADS))

    def z_peer(o):
        return (lax.rem(zed + o, PROMPTS) * 2 + core, me)

    partner = (zed * 2 + 1 - core, me)

    barrier = pltpu.get_barrier_semaphore()

    def greet_head(o, c):
        pl.semaphore_signal(barrier, inc=1, device_id=head_peer(o), device_id_type=MESH)
        return c

    def greet_z(o, c):
        pl.semaphore_signal(barrier, inc=1, device_id=z_peer(o), device_id_type=MESH)
        return c

    lax.fori_loop(1, HEADS, greet_head, 0)
    lax.fori_loop(1, PROMPTS, greet_z, 0)
    pl.semaphore_signal(barrier, inc=1, device_id=partner, device_id_type=MESH)

    def pack_state(o, c):
        s_send[o] = encode(fork_ref[prompt_ref[base + lax.rem(me + o, HEADS)], 0])
        return c

    s_recv[0] = encode(fork_ref[prompt_ref[base + me], 0])
    s_own[...] = fork_ref[prompt_ref[base + me], 0]
    lax.fori_loop(1, HEADS, pack_state, 0)

    row = lax.broadcasted_iota(jnp.int32, (D, D), 0)
    col = lax.broadcasted_iota(jnp.int32, (D, D), 1)
    xor = jnp.where(row < col, jnp.bitwise_xor(row, col), 0)
    for level in range(7):
        m = 1 << level
        mask_s[level] = jnp.where((xor >= m) & (xor < 2 * m), 1.0, 0.0).astype(BF16)
    lower = jnp.where(col <= row, 1.0, 0.0) - jnp.where(col < HALF, 1.0, 0.0)
    tri_s[0] = lower.astype(BF16)
    tri_s[1] = jnp.where(col >= row, 1.0, 0.0).astype(BF16)
    valid = len_ref[base + me]
    keep_lane = jnp.where(lax.broadcasted_iota(jnp.int32, (1, D), 1) < valid, 1.0, 0.0)
    beta_rows = jax.nn.sigmoid(beta_ref[0].astype(F32)) * keep_lane
    beta_pad = cat([beta_rows, jnp.zeros((D - HEADS, D), F32)], 0)
    betat_s[...] = beta_pad
    beta_s[...] = beta_pad.T
    gb_s[...] = jnp.zeros((D, D), F32)

    pl.semaphore_wait(barrier, HEADS - 1 + PROMPTS - 1 + 1)

    def state_copy(o):
        return pltpu.make_async_remote_copy(
            src_ref=s_send.at[o], dst_ref=s_recv.at[o], send_sem=s_ssem.at[o], recv_sem=s_rsem.at[o],
            device_id=head_peer(o), device_id_type=MESH)

    def send_state(o, c):
        state_copy(o).start()
        return c

    lax.fori_loop(1, HEADS, send_state, 0)

    def head_lanes(h):
        return pl.ds(pl.multiple_of(h * D, D), D)

    def beta_column(h):
        return jnp.sum(jnp.where(col == h, beta_s[...], 0.0), axis=1, keepdims=True)

    def keep_rows():
        return lax.broadcasted_iota(jnp.int32, (D, 1), 0) < valid

    def slot_of(h):
        return lax.rem(h - me + HEADS, HEADS)

    def grad_copy(h):
        o = slot_of(h)
        return pltpu.make_async_remote_copy(
            src_ref=ds_send.at[o], dst_ref=ds_recv.at[o], send_sem=d_ssem.at[o], recv_sem=d_rsem.at[o],
            device_id=(grp, h), device_id_type=MESH)

    def unit_parts(h):
        lanes = head_lanes(h)
        q = q_ref[0, :, lanes].astype(F32)
        k = k_ref[0, :, lanes].astype(F32)
        rq = lax.rsqrt(jnp.sum(q * q, axis=1, keepdims=True) + 1e-6)
        rk = lax.rsqrt(jnp.sum(k * k, axis=1, keepdims=True) + 1e-6)
        return q, k, rq, rk

    def masked_grad(h):
        return jnp.where(keep_rows(), do_ref[0, :, head_lanes(h)].astype(F32), 0.0).astype(BF16)

    def decay_rows(h):
        return jnp.where(keep_rows(), g_ref[0, :, head_lanes(h)].astype(F32), 0.0)

    def prepare(h):
        q, k, rq, rk = unit_parts(h)
        uq, uk = q * (rq * SCALE), k * rk
        decay = decay_rows(h)
        cum = dot(tri_s[0], decay.astype(BF16), 1, 0)
        ee = jnp.exp(decay[0:1] - cum[0:1])
        eg = jnp.exp(cum)
        es = jnp.exp(-cum)
        qf, kf = uq * eg, uk * eg
        qfs, kfs, kes = split(qf), split(kf), split(uk * es)
        qts, kts = split(qf * ee), split(kf * ee)
        u_s[h, 0], u_s[h, 1] = uq, uk
        decay_s[h, 0], decay_s[h, 1] = eg, es
        ee_s[h] = jnp.broadcast_to(ee, (8, D))
        for i in range(2):
            qf_s[h, i], kf_s[h, i], ke_s[h, i], kt_s[h, i] = qfs[i], kfs[i], kes[i], kts[i]
        return qfs, kfs, kes, qts, kts

    def couple(h, qfs, kfs, kes):
        both = tuple(cat([kfs[i], qfs[i]], 0) for i in range(2))
        scores = mm3(kes, both, 1, 1)
        beta_row = betat_s[pl.ds(h, 1), :]
        coupling = split(jnp.where(row < col, scores[:, :D] * beta_row, 0.0))
        attend = split(jnp.where(row <= col, scores[:, D:], 0.0))
        return coupling, attend

    def phase_a(hs):
        prep = [prepare(h) for h in hs]
        scores = [couple(h, *p[:3]) for h, p in zip(hs, prep)]
        dos = [masked_grad(h) for h in hs]
        dus = [split(dot(cat([a[0], a[1]], 1), cat([do, do], 0), 1, 0)) for (_, a), do in zip(scores, dos)]
        eye = jnp.where(row == col, 1.0, 0.0)
        invs = [eye - (c[0] * mask_s[0]).astype(F32) - (c[1] * mask_s[0]).astype(F32) for c, _ in scores]
        for level in range(1, 7):
            mask = mask_s[level]
            inv_ps = [split(x) for x in invs]
            steps_f = [mm3((c[0] * mask, c[1] * mask), ip, 1, 0) for (c, _), ip in zip(scores, inv_ps)]
            steps_p = [split(x) for x in steps_f]
            invs = [x - mm3(ip, sp, 1, 0) for x, ip, sp in zip(invs, inv_ps, steps_p)]
        inv_ps = [split(x) for x in invs]
        for h, ip in zip(hs, inv_ps):
            tt_s[h, 0], tt_s[h, 1] = ip
        ws = [mm3(ip, du, 1, 0) for ip, du in zip(inv_ps, dus)]
        nbws = []
        for h, w in zip(hs, ws):
            w_s[h] = w
            nbws.append(split(-(beta_column(h) * w)))
        dss = [
            dot(
                cat([p[3][0], p[3][1], p[4][0], p[4][0], p[4][1]], 0),
                cat([do, do, nbw[0], nbw[1], nbw[0]], 0), 0, 0)
            for p, do, nbw in zip(prep, dos, nbws)]
        for h, ds in zip(hs, dss):
            ds_send[slot_of(h)] = encode(ds)

    def phase_b(hs):
        pair = lambda ref: [(ref[h, 0], ref[h, 1]) for h in hs]
        betas = [beta_column(h) for h in hs]
        kts, tts = pair(kt_s), pair(tt_s)
        sss = []
        for h in hs:
            o = lax.rem(me - h + HEADS, HEADS)
            state = decode(s_recv[o, 0:D], s_recv[o, D : D + TAIL])
            sss.append(split(jnp.where(o == 0, s_own[...], state)))
        reads = [mm3(kt, ss, 1, 0) for kt, ss in zip(kts, sss)]
        targets = [
            split(b * (v_ref[0, :, head_lanes(h)].astype(F32) - r))
            for h, b, r in zip(hs, betas, reads)]
        us = [mm3(tt, tg, 0, 0) for tt, tg in zip(tts, targets)]
        usp = [split(u) for u in us]
        dos = [masked_grad(h) for h in hs]
        nbw_fs = [-(b * w_s[h]) for h, b in zip(hs, betas)]
        nbws = [split(x) for x in nbw_fs]
        dps = [split(jnp.where(row >= col, mm2(do, u, 1, 1), 0.0)) for do, u in zip(dos, usp)]
        dns = [split(jnp.where(row > col, mm3(nbw, u, 1, 1), 0.0)) for nbw, u in zip(nbws, usp)]
        kes, kfs, qfs = pair(ke_s), pair(kf_s), pair(qf_s)
        ees = [ee_s[h][0:1] for h in hs]
        dqfs = [mm2(do, ss, 1, 1) * ee + mm3(dp, ke, 1, 0) for do, ss, ee, dp, ke in zip(dos, sss, ees, dps, kes)]
        dkfs = [mm3(nbw, ss, 1, 1) * ee + mm3(dn, ke, 1, 0) for nbw, ss, ee, dn, ke in zip(nbws, sss, ees, dns, kes)]
        dkes = [
            dot(
                cat([dn[0], dn[0], dn[1], dp[0], dp[0], dp[1]], 0),
                cat([kf[0], kf[1], kf[0], qf[0], qf[1], qf[0]], 0), 0, 0)
            for dn, dp, kf, qf in zip(dns, dps, kfs, qfs)]
        for n, h in enumerate(hs):
            lanes = head_lanes(h)
            keep = keep_rows()
            uq, uk = u_s[h, 0], u_s[h, 1]
            eg, es = decay_s[h, 0], decay_s[h, 1]
            dqg, dkg, dks = dqfs[n] * eg, dkfs[n] * eg, dkes[n] * es
            dc = split(dqg * uq + dkg * uk - dks * uk)
            dg = mm2(tri_s[1], dc, 1, 0)
            gg_ref[0, :, lanes] = jnp.where(keep, dg, 0.0).astype(BF16)
            _, _, rq, rk = unit_parts(h)
            duk = dkg + dks
            gq = rq * (SCALE * dqg - uq * (jnp.sum(uq * dqg, axis=1, keepdims=True) * (1.0 / SCALE)))
            gk = rk * (duk - uk * jnp.sum(uk * duk, axis=1, keepdims=True))
            gq_ref[0, :, lanes] = gq.astype(BF16)
            gk_ref[0, :, lanes] = gk.astype(BF16)
            gv_ref[0, :, lanes] = (-nbw_fs[n]).astype(BF16)
            db = jnp.where(keep, (1.0 - betas[n]) * jnp.sum(w_s[h] * us[n], axis=1, keepdims=True), 0.0)
            gb_s[...] = jnp.where(col == h, db, gb_s[...])

    def loop_a(i, c):
        first = lax.rem(me // HA + i, HEADS // HA) * HA
        phase_a([first + n for n in range(HA)])
        for n in range(HA):
            h = first + n

            @pl.when(h != me)
            def _():
                grad_copy(h).start()

        return c

    lax.fori_loop(0, HEADS // HA, loop_a, 0)

    def wait_state(o, c):
        state_copy(o).wait()
        return c

    lax.fori_loop(1, HEADS, wait_state, 0)

    def pair_copy():
        return pltpu.make_async_remote_copy(
            src_ref=acc.at[1 - core], dst_ref=pair_recv, send_sem=p_ssem, recv_sem=p_rsem,
            device_id=partner, device_id_type=MESH)

    def rs_copy(o):
        return pltpu.make_async_remote_copy(
            src_ref=rs_send.at[lax.rem(zed + o, PROMPTS)], dst_ref=rs_recv.at[o],
            send_sem=r_ssem.at[o], recv_sem=r_rsem.at[o], device_id=z_peer(o), device_id_type=MESH)

    def piece(p, c):
        return ag.at[c, p]

    def ag_copy(o):
        return pltpu.make_async_remote_copy(
            src_ref=piece(zed, core), dst_ref=piece(zed, core),
            send_sem=a_ssem.at[o], recv_sem=a_rsem.at[o], device_id=z_peer(o), device_id_type=MESH)

    def hand_copy(o):
        p = lax.rem(zed - o + PROMPTS, PROMPTS)
        return pltpu.make_async_remote_copy(
            src_ref=piece(p, core), dst_ref=piece(p, core),
            send_sem=f_ssem.at[o], recv_sem=f_rsem.at[o], device_id=partner, device_id_type=MESH)

    def stage_sum():
        def wait_grad(o, c):
            copy = pltpu.make_async_remote_copy(
                src_ref=ds_send.at[o], dst_ref=ds_recv.at[o], send_sem=d_ssem.at[o], recv_sem=d_rsem.at[o],
                device_id=head_peer(o), device_id_type=MESH)
            copy.wait()
            return c

        lax.fori_loop(1, HEADS, wait_grad, 0)

        ds_recv[0] = ds_send[0]
        r64 = lax.broadcasted_iota(jnp.int32, (HALF, D), 0)
        c64 = lax.broadcasted_iota(jnp.int32, (HALF, D), 1)
        source = jnp.zeros((HALF, D), jnp.int32)
        for o in range(HEADS):
            source = jnp.where(c64 // 8 == o, prompt_ref[base + lax.rem(me - o + HEADS, HEADS)], source)
        hit = (source == r64 // 8) & (lax.rem(c64, 8) == lax.rem(r64, 8))
        pick = jnp.where(hit, 1.0, 0.0).astype(BF16)
        pick = cat([pick, pick], 1)

        def sum_rows(r, c):
            half = r // 4
            rows = pl.ds(pl.multiple_of(r * 16, 16), 16)
            parts = [decode(ds_recv[o, rows, :], ds_recv[o, D : D + TAIL, :]) for o in range(HEADS)]
            for n in range(2):
                stack = split(cat([p[8 * n : 8 * n + 8] for p in parts], 0))
                total = dot(pick, cat(stack, 0), 1, 0)
                out_rows = pl.ds(pl.multiple_of(lax.rem(r, 4) * 16 + 8 * n, 8), 8)
                for p in range(PROMPTS):
                    acc[half, p, out_rows, :] = total[8 * p : 8 * p + 8]
            return c

        lax.fori_loop(0, 8, sum_rows, 0)
        pair_copy().start()

    def stage_scatter():
        pair_copy().wait()
        for p in range(PROMPTS):
            both = acc[core, p] + pair_recv[p]
            comb[p] = both
            rs_send[p] = encode(both)
        lax.fori_loop(1, PROMPTS, lambda o, c: (rs_copy(o).start(), c)[1], 0)

    def stage_gather():
        lax.fori_loop(1, PROMPTS, lambda o, c: (rs_copy(o).wait(), c)[1], 0)
        total = comb[zed]
        for o in range(1, PROMPTS):
            total = total + decode(rs_recv[o, 0:HALF], rs_recv[o, HALF : HALF + TAIL])
        ag[core, zed] = encode(total)
        lax.fori_loop(1, PROMPTS, lambda o, c: (ag_copy(o).start(), c)[1], 0)
        hand_copy(0).start()

    def stage_hand():
        def forward(o, c):
            ag_copy(o).wait()
            hand_copy(o).start()
            return c

        lax.fori_loop(1, PROMPTS, forward, 0)

    steps = HEADS // HB
    stages = ((STAGE_SUM, stage_sum), (STAGE_SCATTER, stage_scatter), (STAGE_GATHER, stage_gather), (STAGE_HAND, stage_hand))

    def loop_b(i, c):
        for at, stage in stages:
            if at < steps:
                pl.when(i == at)(stage)
        phase_b([i * HB + n for n in range(HB)])
        return c

    lax.fori_loop(0, steps, loop_b, 0)
    gb_ref[0] = gb_s[...].T[:HEADS].astype(BF16)
    for at, stage in stages:
        if at >= steps:
            stage()
    lax.fori_loop(0, PROMPTS, lambda o, c: (hand_copy(o).wait(), c)[1], 0)
    for p in range(PROMPTS):
        for c in range(2):
            gf_ref[p, 0, HALF * c : HALF * c + HALF] = decode(ag[c, p, 0:HALF], ag[c, p, HALF : HALF + TAIL])


def hand_out(*refs):
    count = (len(refs) - 2) // 3
    ins, outs, bufs = refs[:count], refs[count : 2 * count], refs[2 * count : 3 * count]
    in_sem, out_sem = refs[-2:]

    def load(n):
        return pltpu.make_async_copy(ins[n], bufs[n], in_sem.at[n])

    def save(n):
        return pltpu.make_async_copy(bufs[n], outs[n], out_sem.at[n])

    for n in range(count):
        load(n).start()
    for n in range(count):
        load(n).wait()
        save(n).start()
    for n in range(count):
        save(n).wait()


def pass_on(arrays):
    anywhere = pl.BlockSpec(memory_space=pl.ANY)
    count = len(arrays)
    return pl.pallas_call(
        hand_out,
        out_shape=tuple(jax.ShapeDtypeStruct(a.shape, a.dtype) for a in arrays),
        in_specs=[anywhere] * count,
        out_specs=(anywhere,) * count,
        scratch_shapes=[pltpu.VMEM(a.shape, a.dtype) for a in arrays]
        + [pltpu.SemaphoreType.DMA((count,)), pltpu.SemaphoreType.DMA((count,))],
        name="hand_out",
    )(*arrays)


def per_device(query_rows, key_rows, value_rows, log_decay, beta_logit, out_grad, fork_state, branch_prompt, valid_len):
    vmem = pl.BlockSpec(memory_space=pltpu.VMEM)
    smem = pl.BlockSpec(memory_space=pltpu.SMEM)
    rows = jax.ShapeDtypeStruct(query_rows.shape, BF16)
    dma = pltpu.SemaphoreType.DMA
    pairs = pltpu.VMEM((HEADS, 2, D, D), BF16)
    message = pltpu.VMEM((HEADS, D + TAIL, D), I16)
    beta_rows = beta_logit.transpose(0, 2, 1)
    outs = pl.pallas_call(
        kernel,
        out_shape=(
            rows, rows, rows, rows,
            jax.ShapeDtypeStruct(beta_rows.shape, BF16),
            jax.ShapeDtypeStruct(fork_state.shape, F32),
        ),
        in_specs=[smem, smem] + [vmem] * 7,
        out_specs=(vmem,) * 6,
        scratch_shapes=[
            pltpu.VMEM((D, D), F32),
            message, message, message, message,
            pltpu.VMEM((2, PROMPTS, HALF, D), F32),
            pltpu.VMEM((PROMPTS, HALF, D), F32),
            pltpu.VMEM((PROMPTS, HALF, D), F32),
            pltpu.VMEM((PROMPTS, HALF + TAIL, D), I16),
            pltpu.VMEM((PROMPTS, HALF + TAIL, D), I16),
            pltpu.VMEM((2, PROMPTS, HALF + TAIL, D), I16),
            pltpu.VMEM((HEADS, 2, D, D), F32),
            pltpu.VMEM((HEADS, D, D), F32),
            pltpu.VMEM((HEADS, 2, D, D), F32),
            pltpu.VMEM((HEADS, 8, D), F32),
            pairs, pairs, pairs, pairs, pairs,
            pltpu.VMEM((7, D, D), BF16),
            pltpu.VMEM((2, D, D), BF16),
            pltpu.VMEM((D, D), F32),
            pltpu.VMEM((D, D), F32),
            pltpu.VMEM((D, D), F32),
            dma((HEADS,)), dma((HEADS,)),
            dma((HEADS,)), dma((HEADS,)),
            dma(()), dma(()),
            dma((PROMPTS,)), dma((PROMPTS,)),
            dma((PROMPTS,)), dma((PROMPTS,)),
            dma((PROMPTS,)), dma((PROMPTS,)),
        ],
        compiler_params=pltpu.CompilerParams(collective_id=0, has_side_effects=True),
        name="delta_backward",
    )(branch_prompt, valid_len, query_rows, key_rows, value_rows, log_decay, beta_rows, out_grad, fork_state)
    outs = pass_on(outs)
    return (*outs[:4], outs[4].transpose(0, 2, 1), outs[5])


def solution(mesh):
    branch = P(("grp", "head"), None, None)
    state = P(None, "head", None, None)
    return jax.shard_map(
        per_device,
        mesh=mesh,
        in_specs=(branch,) * 6 + (state, P(), P()),
        out_specs=(branch,) * 5 + (state,),
        check_vma=False,
    )
```

time: 94.6 us -> 51.9 us (0.55)
  Pallas kernels: 84 us -> 51.1 us
  local copies, waits for them, and re-layouts: 9.25 us -> 0 us
    pallas_call x1, Pallas kernels: 84 us -> 48.5 us  [per_device(): pl.pallas_call(kernel, out_shape=(rows, rows, rows, rows, jax.ShapeDtypeS...]
    unnamed x14 -> x0, local copies, waits for them, and re-layouts: 7.83 us -> none
    pallas_call x0 -> x1, Pallas kernels: none -> 2.63 us  [pass_on(): pl.pallas_call(hand_out, out_shape=tuple((jax.ShapeDtypeStruct(a.shape, a...]
    pallas_call x1 -> x0, local copies, waits for them, and re-layouts: 1.42 us -> none  [per_device(): pl.pallas_call(kernel, out_shape=(rows, rows, rows, rows, jax.ShapeDtypeS...]
where the time goes in v2:
time: 51.9 us; the launch traced here: 51.8 us
  Pallas kernels  51.1 us (98%)
  between operations  0.64 us (1%)
    pallas_call x1, Pallas kernels, per_device(): pl.pallas_call(kernel, out_shape=(rows, rows, rows, rows, jax.ShapeDtypeS...  48.5 us
    pallas_call x1, Pallas kernels, pass_on(): pl.pallas_call(hand_out, out_shape=tuple((jax.ShapeDtypeStruct(a.shape, a...  2.63 us

profile of v2, /device:TPU:1, one launch (start us, length us, event | category | flops | bytes accessed | tf_op | source)
XLA Modules:
  0.0 51.8 jit_solution(5965627994688922045)
XLA Ops:
  0.6 48.5 %delta_backward.1 = (bf16[1,128,2048]{2,1,0:T(8,128)(2,1)}, bf16[1,128,2048]{2,1,0:T(8,128)(2,1)}, bf16[1,128,2048]{2,1,0:T(8,128)(2,1)}, bf16[1,128,2048]{2,1,0...) custom-call(s32[256]{0:T(256)} %prompt_ref.1, s32[256]{0:T(256)} %len_ref.1, ...), custom_call_target="tpu_custom_call" | custom-call | tf_op jit(solution)/shard_map/delta_backward/pallas_call | solution.py:436
  49.1 2.6 %hand_out.1 = (bf16[1,128,2048]{2,1,0:T(8,128)(2,1)}, bf16[1,128,2048]{2,1,0:T(8,128)(2,1)}, bf16[1,128,2048]{2,1,0:T(8,128)(2,1)}, bf16[1,128,2048]{2,1,0:T(8,1...) custom-call(bf16[1,128,2048]{2,1,0:T(8,128)(2,1)} %get-tuple-element.18.refs_0_, ...), custom_call_target="tpu_custom_call" | custom-call | tf_op jit(solution)/shard_map/hand_out/pallas_call | solution.py:417

commit v3 on v2

--- a/solution.py
+++ b/solution.py
@@ -17,9 +17,8 @@
 HA = 8
 HB = 4
 TAIL = 16
-STAGE_SUM = 2
-STAGE_SCATTER = 3
-STAGE_GATHER = 4
+STAGE_SUM = 1
+STAGE_GATHER = 3
 STAGE_HAND = 4
 SCALE = D**-0.5
 
@@ -61,9 +60,9 @@
 def kernel(
     prompt_ref, len_ref, q_ref, k_ref, v_ref, g_ref, beta_ref, do_ref, fork_ref,
     gq_ref, gk_ref, gv_ref, gg_ref, gb_ref, gf_ref,
-    s_own, s_send, s_recv, ds_send, ds_recv, acc, pair_recv, comb, rs_send, rs_recv, ag,
+    s_own, s_send, s_recv, ds_send, ds_recv, comb, rs_send, rs_recv, ag,
     u_s, w_s, decay_s, ee_s, qf_s, kf_s, ke_s, kt_s, tt_s, mask_s, tri_s, beta_s, betat_s, gb_s,
-    s_ssem, s_rsem, d_ssem, d_rsem, p_ssem, p_rsem, r_ssem, r_rsem, a_ssem, a_rsem, f_ssem, f_rsem,
+    s_ssem, s_rsem, d_ssem, d_rsem, r_ssem, r_rsem, a_ssem, a_rsem, f_ssem, f_rsem,
 ):
     grp = lax.axis_index("grp")
     me = lax.axis_index("head")
@@ -74,6 +73,9 @@
     def head_peer(o):
         return (grp, lax.rem(me + o, HEADS))
 
+    def chip_peer(o, x):
+        return (zed * 2 + x, lax.rem(me + o, HEADS))
+
     def z_peer(o):
         return (lax.rem(zed + o, PROMPTS) * 2 + core, me)
 
@@ -82,7 +84,8 @@
     barrier = pltpu.get_barrier_semaphore()
 
     def greet_head(o, c):
-        pl.semaphore_signal(barrier, inc=1, device_id=head_peer(o), device_id_type=MESH)
+        for x in range(2):
+            pl.semaphore_signal(barrier, inc=1, device_id=chip_peer(o, x), device_id_type=MESH)
         return c
 
     def greet_z(o, c):
@@ -118,7 +121,7 @@
     beta_s[...] = beta_pad.T
     gb_s[...] = jnp.zeros((D, D), F32)
 
-    pl.semaphore_wait(barrier, HEADS - 1 + PROMPTS - 1 + 1)
+    pl.semaphore_wait(barrier, 2 * (HEADS - 1) + PROMPTS - 1 + 1)
 
     def state_copy(o):
         return pltpu.make_async_remote_copy(
@@ -143,11 +146,11 @@
     def slot_of(h):
         return lax.rem(h - me + HEADS, HEADS)
 
-    def grad_copy(h):
+    def grad_copy(h, x):
         o = slot_of(h)
         return pltpu.make_async_remote_copy(
-            src_ref=ds_send.at[o], dst_ref=ds_recv.at[o], send_sem=d_ssem.at[o], recv_sem=d_rsem.at[o],
-            device_id=(grp, h), device_id_type=MESH)
+            src_ref=ds_send.at[o, x], dst_ref=ds_recv.at[o, core], send_sem=d_ssem.at[o, x], recv_sem=d_rsem.at[o, core],
+            device_id=(zed * 2 + x, h), device_id_type=MESH)
 
     def unit_parts(h):
         lanes = head_lanes(h)
@@ -199,6 +202,26 @@
         for level in range(1, 7):
             mask = mask_s[level]
             inv_ps = [split(x) for x in invs]
+            size = 1 << level
+            if size >= 16:
+                spots = range(0, D, 2 * size)
+                even = lambda x: cat([x[r : r + size] for r in spots], 0)
+                gap = jnp.zeros((size, D), BF16)
+
+                def spread(x):
+                    return cat([y for n in range(len(spots)) for y in (x[n * size : (n + 1) * size], gap)], 0)
+
+                masked = even(mask)
+                steps_f = [
+                    mm3((even(c[0]) * masked, even(c[1]) * masked), ip, 1, 0)
+                    for (c, _), ip in zip(scores, inv_ps)]
+                steps_p = [tuple(spread(y) for y in split(x)) for x in steps_f]
+                outs = [mm3((even(ip[0]), even(ip[1])), sp, 1, 0) for ip, sp in zip(inv_ps, steps_p)]
+                invs = [
+                    cat([y for n, r in enumerate(spots) for y in (
+                        x[r : r + size] - z[n * size : (n + 1) * size], x[r + size : r + 2 * size])], 0)
+                    for x, z in zip(invs, outs)]
+                continue
             steps_f = [mm3((c[0] * mask, c[1] * mask), ip, 1, 0) for (c, _), ip in zip(scores, inv_ps)]
             steps_p = [split(x) for x in steps_f]
             invs = [x - mm3(ip, sp, 1, 0) for x, ip, sp in zip(invs, inv_ps, steps_p)]
@@ -216,7 +239,8 @@
                 cat([do, do, nbw[0], nbw[1], nbw[0]], 0), 0, 0)
             for p, do, nbw in zip(prep, dos, nbws)]
         for h, ds in zip(hs, dss):
-            ds_send[slot_of(h)] = encode(ds)
+            for x in range(2):
+                ds_send[slot_of(h), x] = encode(ds[HALF * x : HALF * x + HALF])
 
     def phase_b(hs):
         pair = lambda ref: [(ref[h, 0], ref[h, 1]) for h in hs]
@@ -267,14 +291,16 @@
             gb_s[...] = jnp.where(col == h, db, gb_s[...])
 
     def loop_a(i, c):
-        first = lax.rem(me // HA + i, HEADS // HA) * HA
+        first = lax.rem(me // HA + i + 1, HEADS // HA) * HA
         phase_a([first + n for n in range(HA)])
         for n in range(HA):
             h = first + n
 
-            @pl.when(h != me)
-            def _():
-                grad_copy(h).start()
+            for x in range(2):
+
+                @pl.when((h != me) | (core != x))
+                def _():
+                    grad_copy(h, x).start()
 
         return c
 
@@ -285,11 +311,6 @@
         return c
 
     lax.fori_loop(1, HEADS, wait_state, 0)
-
-    def pair_copy():
-        return pltpu.make_async_remote_copy(
-            src_ref=acc.at[1 - core], dst_ref=pair_recv, send_sem=p_ssem, recv_sem=p_rsem,
-            device_id=partner, device_id_type=MESH)
 
     def rs_copy(o):
         return pltpu.make_async_remote_copy(
@@ -312,45 +333,45 @@
 
     def stage_sum():
         def wait_grad(o, c):
-            copy = pltpu.make_async_remote_copy(
-                src_ref=ds_send.at[o], dst_ref=ds_recv.at[o], send_sem=d_ssem.at[o], recv_sem=d_rsem.at[o],
-                device_id=head_peer(o), device_id_type=MESH)
-            copy.wait()
+            for x in range(2):
+
+                @pl.when((o != 0) | (core != x))
+                def _():
+                    pltpu.make_async_remote_copy(
+                        src_ref=ds_send.at[o, x], dst_ref=ds_recv.at[o, x], send_sem=d_ssem.at[o, x],
+                        recv_sem=d_rsem.at[o, x], device_id=chip_peer(o, x), device_id_type=MESH).wait()
+
             return c
 
-        lax.fori_loop(1, HEADS, wait_grad, 0)
-
-        ds_recv[0] = ds_send[0]
-        r64 = lax.broadcasted_iota(jnp.int32, (HALF, D), 0)
-        c64 = lax.broadcasted_iota(jnp.int32, (HALF, D), 1)
-        source = jnp.zeros((HALF, D), jnp.int32)
-        for o in range(HEADS):
-            source = jnp.where(c64 // 8 == o, prompt_ref[base + lax.rem(me - o + HEADS, HEADS)], source)
+        lax.fori_loop(0, HEADS, wait_grad, 0)
+        ds_recv[0, core] = ds_send[0, core]
+        wide = 2 * HEADS * 8
+        r64 = lax.broadcasted_iota(jnp.int32, (HALF, wide), 0)
+        c64 = lax.broadcasted_iota(jnp.int32, (HALF, wide), 1)
+        source = jnp.zeros((HALF, wide), jnp.int32)
+        for n in range(2 * HEADS):
+            branch = (zed * 2 + n % 2) * HEADS + lax.rem(me - n // 2 + HEADS, HEADS)
+            source = jnp.where(c64 // 8 == n, prompt_ref[branch], source)
         hit = (source == r64 // 8) & (lax.rem(c64, 8) == lax.rem(r64, 8))
         pick = jnp.where(hit, 1.0, 0.0).astype(BF16)
         pick = cat([pick, pick], 1)
 
         def sum_rows(r, c):
-            half = r // 4
             rows = pl.ds(pl.multiple_of(r * 16, 16), 16)
-            parts = [decode(ds_recv[o, rows, :], ds_recv[o, D : D + TAIL, :]) for o in range(HEADS)]
+            parts = [
+                decode(ds_recv[n // 2, n % 2, rows, :], ds_recv[n // 2, n % 2, HALF : HALF + TAIL, :])
+                for n in range(2 * HEADS)]
             for n in range(2):
                 stack = split(cat([p[8 * n : 8 * n + 8] for p in parts], 0))
                 total = dot(pick, cat(stack, 0), 1, 0)
-                out_rows = pl.ds(pl.multiple_of(lax.rem(r, 4) * 16 + 8 * n, 8), 8)
+                out_rows = pl.ds(pl.multiple_of(r * 16 + 8 * n, 8), 8)
                 for p in range(PROMPTS):
-                    acc[half, p, out_rows, :] = total[8 * p : 8 * p + 8]
+                    comb[p, out_rows, :] = total[8 * p : 8 * p + 8]
             return c
 
-        lax.fori_loop(0, 8, sum_rows, 0)
-        pair_copy().start()
-
-    def stage_scatter():
-        pair_copy().wait()
+        lax.fori_loop(0, HALF // 16, sum_rows, 0)
         for p in range(PROMPTS):
-            both = acc[core, p] + pair_recv[p]
-            comb[p] = both
-            rs_send[p] = encode(both)
+            rs_send[p] = encode(comb[p])
         lax.fori_loop(1, PROMPTS, lambda o, c: (rs_copy(o).start(), c)[1], 0)
 
     def stage_gather():
@@ -371,7 +392,7 @@
         lax.fori_loop(1, PROMPTS, forward, 0)
 
     steps = HEADS // HB
-    stages = ((STAGE_SUM, stage_sum), (STAGE_SCATTER, stage_scatter), (STAGE_GATHER, stage_gather), (STAGE_HAND, stage_hand))
+    stages = ((STAGE_SUM, stage_sum), (STAGE_GATHER, stage_gather), (STAGE_HAND, stage_hand))
 
     def loop_b(i, c):
         for at, stage in stages:
@@ -432,6 +453,7 @@
     dma = pltpu.SemaphoreType.DMA
     pairs = pltpu.VMEM((HEADS, 2, D, D), BF16)
     message = pltpu.VMEM((HEADS, D + TAIL, D), I16)
+    halves = pltpu.VMEM((HEADS, 2, HALF + TAIL, D), I16)
     beta_rows = beta_logit.transpose(0, 2, 1)
     outs = pl.pallas_call(
         kernel,
@@ -444,9 +466,7 @@
         out_specs=(vmem,) * 6,
         scratch_shapes=[
             pltpu.VMEM((D, D), F32),
-            message, message, message, message,
-            pltpu.VMEM((2, PROMPTS, HALF, D), F32),
-            pltpu.VMEM((PROMPTS, HALF, D), F32),
+            message, message, halves, halves,
             pltpu.VMEM((PROMPTS, HALF, D), F32),
             pltpu.VMEM((PROMPTS, HALF + TAIL, D), I16),
             pltpu.VMEM((PROMPTS, HALF + TAIL, D), I16),
@@ -462,8 +482,7 @@
             pltpu.VMEM((D, D), F32),
             pltpu.VMEM((D, D), F32),
             dma((HEADS,)), dma((HEADS,)),
-            dma((HEADS,)), dma((HEADS,)),
-            dma(()), dma(()),
+            dma((HEADS, 2)), dma((HEADS, 2)),
             dma((PROMPTS,)), dma((PROMPTS,)),
             dma((PROMPTS,)), dma((PROMPTS,)),
             dma((PROMPTS,)), dma((PROMPTS,)),

time: 51.9 us -> 49.9 us (0.961)
  Pallas kernels: 51.1 us -> 49.1 us
    pallas_call x1, Pallas kernels: 48.5 us -> 46.5 us  [per_device(): pl.pallas_call(kernel, out_shape=(rows, rows, rows, rows, jax.ShapeDtypeS...]
where the time goes in v3:
time: 49.9 us; the launch traced here: 49.8 us
  Pallas kernels  49.1 us (98%)
  between operations  0.64 us (1%)
    pallas_call x1, Pallas kernels, per_device(): pl.pallas_call(kernel, out_shape=(rows, rows, rows, rows, jax.ShapeDtypeS...  46.5 us
    pallas_call x1, Pallas kernels, pass_on(): pl.pallas_call(hand_out, out_shape=tuple((jax.ShapeDtypeStruct(a.shape, a...  2.63 us

profile of v3, /device:TPU:1, one launch (start us, length us, event | category | flops | bytes accessed | tf_op | source)
XLA Modules:
  0.0 49.8 jit_solution(10940733988365873270)
XLA Ops:
  0.6 46.5 %delta_backward.1 = (bf16[1,128,2048]{2,1,0:T(8,128)(2,1)}, bf16[1,128,2048]{2,1,0:T(8,128)(2,1)}, bf16[1,128,2048]{2,1,0:T(8,128)(2,1)}, bf16[1,128,2048]{2,1,0...) custom-call(s32[256]{0:T(256)} %prompt_ref.1, s32[256]{0:T(256)} %len_ref.1, ...), custom_call_target="tpu_custom_call" | custom-call | tf_op jit(solution)/shard_map/delta_backward/pallas_call | solution.py:458
  47.1 2.6 %hand_out.1 = (bf16[1,128,2048]{2,1,0:T(8,128)(2,1)}, bf16[1,128,2048]{2,1,0:T(8,128)(2,1)}, bf16[1,128,2048]{2,1,0:T(8,128)(2,1)}, bf16[1,128,2048]{2,1,0:T(8,1...) custom-call(bf16[1,128,2048]{2,1,0:T(8,128)(2,1)} %get-tuple-element.18.refs_0_, ...), custom_call_target="tpu_custom_call" | custom-call | tf_op jit(solution)/shard_map/hand_out/pallas_call | solution.py:438
